TPU v7x, 32 devices: a whole 2x2x4 slice. The times are simulated.
32 devices in a mesh: band: 2 (over y), coarse: 4 (over x, core), fine: 4 (over z).
Axes of the slice: x: 2, y: 2, z: 4, core: 2. Of those that a mesh axis runs over, the one named last changes fastest.
Arguments:
- spectra: float32 [32, 8, 8192], P(None, ('band', 'coarse'), 'fine'), parts along dimension 1, may hold values from 0.2 to 5
Outputs:
- drift_power: float32 [8, 32, 8, 8192], P(None, None, ('band', 'coarse'), 'fine'), parts along dimension 2
There are 2 independent parts, one for each index of `band`. A program takes and returns all parts, laid end to end along the dimension named above; each array names one. Nothing has to cross between parts.
All inputs are finite; a program needn't handle non-finite values.
Results may differ from a plain program's by a relative error of at most 0.00002.
Values sent between devices are 32-bit elements; how exact they have to be, the bound alone decides.
A program may use at most 64 MiB of HBM per device.

v0:
```python
import functools

import jax
import jax.numpy as jnp
from jax import lax
from jax.experimental import pallas as pl
from jax.experimental.pallas import tpu as pltpu
from jax.sharding import PartitionSpec as P

RATES = 8
LANES = 128
PIECES = 4
UNROLL = 2
ROW = 18
HEAD = 1
MESH = pl.DeviceIdType.MESH


def comm_kernel(
    channels, fines, rows, chunks, x_ref, e_ref,
    edge, hraw, part_a, sum_1, part_b, inv_1, part_c, halo_a, halo_1, halo_b, halo_i, halo_c,
    edge_send, edge_recv, a_send, a_recv, b_send, b_recv, c_send, c_recv,
):
    half_rows = rows // 2
    piece_rows = half_rows // PIECES
    size = piece_rows * chunks
    others = channels // 2 - 1
    c = lax.axis_index("coarse")
    f = lax.axis_index("fine")
    mine = c % 2
    pair = c // 2
    partner = {"coarse": pair * 2 + 1 - mine}
    peers = [{"coarse": ((pair + o) % (channels // 2)) * 2 + mine} for o in range(1, others + 1)]
    place = c * fines + f
    after = (place + 1) % (channels * fines)
    before = (place + channels * fines - 1) % (channels * fines)
    after_id = {"coarse": after // fines, "fine": after % fines}
    before_id = {"coarse": before // fines, "fine": before % fines}

    barrier = pltpu.get_barrier_semaphore()
    greet = [partner] + peers + [after_id, before_id]
    for device in greet:
        pl.semaphore_signal(barrier, inc=1, device_id=device, device_id_type=MESH)
    for half in range(2):
        start = half * half_rows * chunks
        edge[0, half] = x_ref[pl.ds(start + chunks - 1, half_rows, stride=chunks), :]
        edge[1, half] = x_ref[pl.ds(start, half_rows, stride=chunks), :]
    pl.semaphore_wait(barrier, len(greet))

    started = []

    def send(src, dst, send_sem, recv_sem, device):
        copy = pltpu.make_async_remote_copy(
            src_ref=src, dst_ref=dst, send_sem=send_sem, recv_sem=recv_sem,
            device_id=device, device_id_type=MESH,
        )
        copy.start()
        started.append(copy)
        return copy

    def piece_start(half, p):
        return pl.multiple_of((half * half_rows + p * piece_rows) * chunks, 8)

    halos = [
        send(edge.at[0], hraw.at[0], edge_send.at[0], edge_recv.at[0], after_id),
        send(edge.at[1], hraw.at[1], edge_send.at[1], edge_recv.at[1], before_id),
    ]
    theirs = 1 - mine
    a_copies = [
        send(x_ref.at[pl.ds(piece_start(theirs, p), size), :], part_a.at[p], a_send.at[p], a_recv.at[p], partner)
        for p in range(PIECES)
    ]
    b_copies = []
    for p in range(PIECES):
        a_copies[p].wait_recv()
        sum_1[p] = x_ref[pl.ds(piece_start(mine, p), size), :] + part_a[p]
        b_copies.append([
            send(sum_1.at[p], part_b.at[o, p], b_send.at[o, p], b_recv.at[o, p], peers[o])
            for o in range(others)
        ])
    for copy in halos:
        copy.wait_recv()
    halo_pair = [
        send(hraw.at[side, theirs], halo_a.at[side], a_send.at[PIECES + side], a_recv.at[PIECES + side], partner)
        for side in range(2)
    ]
    for side in range(2):
        halo_pair[side].wait_recv()
        halo_1[side] = hraw[side, mine] + halo_a[side]
    halo_b_copies = [
        send(halo_1, halo_b.at[o], b_send.at[o, PIECES], b_recv.at[o, PIECES], peers[o])
        for o in range(others)
    ]

    def put(half, p, inverse):
        normed = x_ref[pl.ds(piece_start(half, p), size), :] * inverse - 1.0
        for i in range(piece_rows):
            t = half * half_rows + p * piece_rows + i
            e_ref[pl.ds(t * ROW + HEAD, chunks), :] = normed[i * chunks : (i + 1) * chunks]

    c_copies = []
    for p in range(PIECES):
        total = sum_1[p]
        for o in range(others):
            b_copies[p][o].wait_recv()
            total = total + part_b[o, p]
        inv_1[p] = 1.0 / (total / channels)
        c_copies.append(send(inv_1.at[p], part_c.at[p], c_send.at[p], c_recv.at[p], partner))
        put(mine, p, inv_1[p])
    total = halo_1[...]
    for o in range(others):
        halo_b_copies[o].wait_recv()
        total = total + halo_b[o]
    halo_i[...] = 1.0 / (total / channels)
    halo_c_copy = send(halo_i, halo_c, c_send.at[PIECES], c_recv.at[PIECES], partner)

    at_edge = [place == 0, place == channels * fines - 1]
    at_row = [HEAD - 1, HEAD + chunks]

    def put_halo(half, inverse):
        for side in range(2):
            normed = hraw[side, half] * inverse[side] - 1.0
            normed = jnp.where(at_edge[side], jnp.zeros_like(normed), normed)
            for i in range(half_rows):
                t = half * half_rows + i
                e_ref[pl.ds(t * ROW + at_row[side], 1), :] = normed[i : i + 1]

    put_halo(mine, halo_i)
    for p in range(PIECES):
        c_copies[p].wait_recv()
        put(theirs, p, part_c[p])
    halo_c_copy.wait_recv()
    put_halo(theirs, halo_c)
    for copy in started:
        copy.wait_send()


def tree_kernel(channels, fines, rows, chunks, e_ref, out_hbm, out, halo, *rest):
    levels = (None,) + rest[:-1]
    out_sem = rest[-1]
    depth = len(levels)
    last = jnp.logical_and(
        lax.axis_index("coarse") == channels - 1, lax.axis_index("fine") == fines - 1
    )
    lane = lax.broadcasted_iota(jnp.int32, (chunks, LANES), 1)
    chunk = lax.broadcasted_iota(jnp.int32, (chunks, LANES), 0)
    final = chunk == chunks - 1
    edge = jnp.logical_and(jnp.logical_and(final, lane == LANES - 1), last)
    lane_q = lax.broadcasted_iota(jnp.int32, (RATES, LANES), 1)
    slope_q = RATES - 1 - RATES // 2 - lax.broadcasted_iota(jnp.int32, (RATES, LANES), 0)

    def at(q, row):
        return (q * rows + row) * chunks

    def left(value, amount):
        return value if amount % LANES == 0 else pltpu.roll(value, -amount % LANES, 1)

    for t in range(rows):
        base = t * ROW + HEAD + chunks
        inner = jnp.broadcast_to(e_ref[pl.ds(base - 1, 1), :], (RATES, LANES))
        outer = jnp.broadcast_to(e_ref[pl.ds(base, 1), :], (RATES, LANES))
        value = jnp.where(lane_q >= slope_q * t + LANES, inner, outer)
        value = left(value, (RATES - 1 - RATES // 2) * t)
        for part in (t // 2, t - t // 2):
            if part:
                value = pltpu.roll(value, 0, 1, stride=part, stride_axis=0)
        halo[0, t] = jnp.where(last, jnp.zeros_like(value), value)
    for level in range(depth - 1):
        m = 1 << level
        for r in range(rows // (2 * m)):
            for d in range(m):
                first = halo[level, 2 * r * m + d]
                second = halo[level, (2 * r + 1) * m + d]
                for odd in range(2):
                    halo[level + 1, r * 2 * m + 2 * d + odd] = first + left(second, d + odd)

    def windows(t):
        return [e_ref[pl.ds(t * ROW + HEAD + shift, chunks), :] for shift in (-1, 0, 1)]

    def shifted(seen, amount):
        down = 1 if amount >= 0 else 0
        lanes = amount % LANES
        if lanes == 0:
            return seen[down + (amount - lanes) // LANES + 1 - down]
        return left(jnp.where(lane >= lanes, seen[down], seen[down + 1]), lanes)

    for r in range(rows // 2):
        even, odd_row = windows(2 * r), windows(2 * r + 1)
        for q in range(RATES):
            slope = q - RATES // 2
            first = shifted(even, slope * 2 * r)
            second = shifted(odd_row, slope * (2 * r + 1))
            ahead = shifted(odd_row, slope * (2 * r + 1) + 1)
            ahead = jnp.where(edge, jnp.zeros_like(ahead), ahead)
            levels[1][pl.ds(at(q, 2 * r), chunks), :] = first + second
            levels[1][pl.ds(at(q, 2 * r + 1), chunks), :] = first + ahead

    def tree(step, carry):
        for level in range(1, depth):
            m = 1 << level
            source = levels[level]
            for r in range(rows // (2 * m)):
                for d in range(m):
                    for sub in range(UNROLL):
                        q = step * UNROLL + sub
                        row_b = (2 * r + 1) * m + d
                        where_b = pl.multiple_of(at(q, row_b), 8)
                        first = source[pl.ds(pl.multiple_of(at(q, 2 * r * m + d), 8), chunks), :]
                        second = source[pl.ds(where_b, chunks), :]
                        ahead = source[pl.ds(where_b + 1, chunks), :]
                        beyond = jnp.broadcast_to(halo[level, row_b, pl.ds(RATES - 1 - q, 1), :], (chunks, LANES))
                        ahead = jnp.where(final, beyond, ahead)
                        for odd in range(2):
                            k = d + odd
                            moved = second
                            if k:
                                moved = left(jnp.where(lane >= k, second, ahead), k)
                            row = r * 2 * m + 2 * d + odd
                            value = first + moved
                            if level + 1 < depth:
                                levels[level + 1][pl.ds(pl.multiple_of(at(q, row), 8), chunks), :] = value
                            else:
                                out[q, row * chunks : (row + 1) * chunks] = value
        for sub in range(UNROLL):
            q = step * UNROLL + sub
            pltpu.make_async_copy(out.at[q], out_hbm.at[q], out_sem.at[q]).start()
        return carry

    lax.fori_loop(0, RATES // UNROLL, tree, 0)
    for q in range(RATES):
        pltpu.make_async_copy(out.at[q], out_hbm.at[q], out_sem.at[q]).wait()


def on_device(channels, fines, spectra):
    rows, _, columns = spectra.shape
    chunks = columns // LANES
    depth = rows.bit_length() - 1
    assert (RATES // 2) * (rows - 1) <= LANES and rows == 1 << depth
    others = channels // 2 - 1
    half = rows // 2
    size = half // PIECES * chunks
    vmem = functools.partial(pltpu.VMEM, dtype=jnp.float32)
    dma = pltpu.SemaphoreType.DMA
    x = spectra.reshape(rows * chunks, LANES)
    normed = pl.pallas_call(
        functools.partial(comm_kernel, channels, fines, rows, chunks),
        out_shape=jax.ShapeDtypeStruct((rows * ROW, LANES), jnp.float32),
        in_specs=[pl.BlockSpec(memory_space=pltpu.VMEM)],
        out_specs=pl.BlockSpec(memory_space=pltpu.VMEM),
        scratch_shapes=[
            vmem((2, 2, half, LANES)), vmem((2, 2, half, LANES)),
            vmem((PIECES, size, LANES)), vmem((PIECES, size, LANES)),
            vmem((others, PIECES, size, LANES)), vmem((PIECES, size, LANES)), vmem((PIECES, size, LANES)),
            vmem((2, half, LANES)), vmem((2, half, LANES)), vmem((others, 2, half, LANES)),
            vmem((2, half, LANES)), vmem((2, half, LANES)),
            dma((2,)), dma((2,)), dma((PIECES + 2,)), dma((PIECES + 2,)),
            dma((others, PIECES + 1)), dma((others, PIECES + 1)), dma((PIECES + 1,)), dma((PIECES + 1,)),
        ],
        compiler_params=pltpu.CompilerParams(collective_id=0, has_side_effects=True),
        name="normalize",
    )(x)
    stored = RATES * rows * chunks + 8
    out = pl.pallas_call(
        functools.partial(tree_kernel, channels, fines, rows, chunks),
        out_shape=jax.ShapeDtypeStruct((RATES, rows * chunks, LANES), jnp.float32),
        in_specs=[pl.BlockSpec(memory_space=pltpu.VMEM)],
        out_specs=pl.BlockSpec(memory_space=pl.ANY),
        scratch_shapes=[vmem((RATES, rows * chunks, LANES)), vmem((depth, rows, RATES, LANES))]
        + [vmem((stored, LANES))] * (depth - 1)
        + [dma((RATES,))],
        compiler_params=pltpu.CompilerParams(vmem_limit_bytes=48 << 20),
        name="tree",
    )(normed)
    return out.reshape(RATES, rows, 1, columns)


def solution(mesh):
    body = functools.partial(on_device, mesh.shape["coarse"], mesh.shape["fine"])
    in_specs = (P(None, ("band", "coarse"), "fine"),)
    out_specs = P(None, None, ("band", "coarse"), "fine")
    return jax.shard_map(body, mesh=mesh, in_specs=in_specs, out_specs=out_specs, check_vma=False)
```

profile of v0, /device:TPU:0, one launch (start us, length us, event | category | flops | bytes accessed | tf_op | source)
XLA Modules:
  0.0 19.3 jit_solution(10138210001403069156)
XLA Ops:
  0.0 14.1 %normalize.1.e_ref = f32[576,128]{1,0:T(8,128)} custom-call(f32[512,128]{1,0:T(8,128)} %bitcast.2), custom_call_target="tpu_custom_call" | custom-call | tf_op jit(solution)/shard_map/normalize/pallas_call | solution.py:245
  14.2 0.0 copy-start
  14.2 1.0 %copy-done = f32[576,128]{1,0:T(8,128)S(1)} copy-done((f32[576,128]{1,0:T(8,128)S(1)}, f32[576,128]{1,0:T(8,128)}, u32[]{:S(2)}) %copy-start) | copy-done | bytes 294936
  15.1 4.2 %tree.1 = f32[8,512,128]{2,1,0:T(8,128)} custom-call(f32[576,128]{1,0:T(8,128)S(1)} %copy-done), custom_call_target="tpu_custom_call" | custom-call | tf_op jit(solution)/shard_map/tree/pallas_call | solution.py:263
Async XLA Ops:
  14.2 1.0 %copy-start = (f32[576,128]{1,0:T(8,128)S(1)}, f32[576,128]{1,0:T(8,128)}, u32[]{:S(2)}) copy-start(f32[576,128]{1,0:T(8,128)} %normalize.1.e_ref) | copy-start | bytes 884740
where the time goes:
time: 19.5 us; the launch traced here: 19.3 us
  Pallas kernels  18.3 us (94%)
  local copies, waits for them, and re-layouts  0.95 us (5%)
    pallas_call x1, Pallas kernels, on_device(): pl.pallas_call(functools.partial(comm_kernel, channels, fines, rows, chun...  14.1 us
    pallas_call x1, Pallas kernels, on_device(): pl.pallas_call(functools.partial(tree_kernel, channels, fines, rows, chun...  4.18 us
    unnamed x2, local copies, waits for them, and re-layouts  0.95 us

commit v1 on v0

--- a/solution.py
+++ b/solution.py
@@ -256,7 +256,7 @@
             dma((2,)), dma((2,)), dma((PIECES + 2,)), dma((PIECES + 2,)),
             dma((others, PIECES + 1)), dma((others, PIECES + 1)), dma((PIECES + 1,)), dma((PIECES + 1,)),
         ],
-        compiler_params=pltpu.CompilerParams(collective_id=0, has_side_effects=True),
+        compiler_params=pltpu.CompilerParams(collective_id=0, has_side_effects=True, vmem_limit_bytes=8 << 20),
         name="normalize",
     )(x)
     stored = RATES * rows * chunks + 8
@@ -268,7 +268,7 @@
         scratch_shapes=[vmem((RATES, rows * chunks, LANES)), vmem((depth, rows, RATES, LANES))]
         + [vmem((stored, LANES))] * (depth - 1)
         + [dma((RATES,))],
-        compiler_params=pltpu.CompilerParams(vmem_limit_bytes=48 << 20),
+        compiler_params=pltpu.CompilerParams(vmem_limit_bytes=20 << 20),
         name="tree",
     )(normed)
     return out.reshape(RATES, rows, 1, columns)

time: 19.5 us -> 17.8 us (0.913)
  Pallas kernels: 18.3 us -> 16.7 us
    pallas_call x1, Pallas kernels: 14.1 us -> 12.5 us  [on_device(): pl.pallas_call(functools.partial(comm_kernel, channels, fines, rows, chun...]
where the time goes in v1:
time: 17.8 us; the launch traced here: 17.6 us
  Pallas kernels  16.7 us (94%)
  local copies, waits for them, and re-layouts  0.95 us (5%)
    pallas_call x1, Pallas kernels, on_device(): pl.pallas_call(functools.partial(comm_kernel, channels, fines, rows, chun...  12.5 us
    pallas_call x1, Pallas kernels, on_device(): pl.pallas_call(functools.partial(tree_kernel, channels, fines, rows, chun...  4.18 us
    unnamed x2, local copies, waits for them, and re-layouts  0.95 us

profile of v1, /device:TPU:0, one launch (start us, length us, event | category | flops | bytes accessed | tf_op | source)
XLA Modules:
  0.0 17.6 jit_solution(3454449301947086013)
XLA Ops:
  0.0 0.0 copy-start
  0.0 0.9 %copy-done = f32[32,1,2048]{2,1,0:T(1,128)S(1)} copy-done((f32[32,1,2048]{2,1,0:T(1,128)S(1)}, f32[32,1,2048]{2,1,0:T(1,128)}, u32[]{:S(2)}) %copy-start) | copy-done | bytes 262168
  1.0 12.5 %normalize.1.e_ref = f32[576,128]{1,0:T(8,128)S(1)} custom-call(f32[512,128]{1,0:T(8,128)S(1)} %bitcast.2), custom_call_target="tpu_custom_call" | custom-call | tf_op jit(solution)/shard_map/normalize/pallas_call | solution.py:245
  13.4 4.2 %tree.1 = f32[8,512,128]{2,1,0:T(8,128)} custom-call(f32[576,128]{1,0:T(8,128)S(1)} %normalize.1.e_ref), custom_call_target="tpu_custom_call" | custom-call | tf_op jit(solution)/shard_map/tree/pallas_call | solution.py:263
Async XLA Ops:
  0.0 0.9 %copy-start = (f32[32,1,2048]{2,1,0:T(1,128)S(1)}, f32[32,1,2048]{2,1,0:T(1,128)}, u32[]{:S(2)}) copy-start(f32[32,1,2048]{2,1,0:T(1,128)} %param.1) | copy-start | bytes 786436

commit v2 on v1

--- a/solution.py
+++ b/solution.py
@@ -17,9 +17,9 @@
 
 
 def comm_kernel(
-    channels, fines, rows, chunks, x_ref, e_ref,
-    edge, hraw, part_a, sum_1, part_b, inv_1, part_c, halo_a, halo_1, halo_b, halo_i, halo_c,
-    edge_send, edge_recv, a_send, a_recv, b_send, b_recv, c_send, c_recv,
+    channels, fines, rows, chunks, x_hbm, e_ref,
+    x_ref, edge, edge_a, edge_1, edge_b, edge_n, halo, part_a, sum_1, part_b, inv_1, part_c,
+    x_sem, a_send, a_recv, b_send, b_recv, c_send, c_recv, h_send, h_recv, ready,
 ):
     half_rows = rows // 2
     piece_rows = half_rows // PIECES
@@ -28,24 +28,47 @@
     c = lax.axis_index("coarse")
     f = lax.axis_index("fine")
     mine = c % 2
+    theirs = 1 - mine
     pair = c // 2
-    partner = {"coarse": pair * 2 + 1 - mine}
+    next_c = (c + 1) % channels
+    prev_c = (c + channels - 1) % channels
+    partner = {"coarse": pair * 2 + theirs}
     peers = [{"coarse": ((pair + o) % (channels // 2)) * 2 + mine} for o in range(1, others + 1)]
     place = c * fines + f
     after = (place + 1) % (channels * fines)
     before = (place + channels * fines - 1) % (channels * fines)
-    after_id = {"coarse": after // fines, "fine": after % fines}
-    before_id = {"coarse": before // fines, "fine": before % fines}
-
+    around = [
+        {"coarse": after // fines, "fine": after % fines},
+        {"coarse": before // fines, "fine": before % fines},
+    ]
+
+    def signal(sem, **device):
+        pl.semaphore_signal(sem, inc=1, device_id=device, device_id_type=MESH)
+
+    fetch = pltpu.make_async_copy(x_hbm, x_ref, x_sem)
+    fetch.start()
     barrier = pltpu.get_barrier_semaphore()
-    greet = [partner] + peers + [after_id, before_id]
-    for device in greet:
-        pl.semaphore_signal(barrier, inc=1, device_id=device, device_id_type=MESH)
-    for half in range(2):
-        start = half * half_rows * chunks
-        edge[0, half] = x_ref[pl.ds(start + chunks - 1, half_rows, stride=chunks), :]
-        edge[1, half] = x_ref[pl.ds(start, half_rows, stride=chunks), :]
-    pl.semaphore_wait(barrier, len(greet))
+    for o in range(1, channels):
+        signal(barrier, coarse=(c + o) % channels)
+
+    @pl.when(f > 0)
+    def _():
+        signal(barrier, fine=f - 1)
+
+    @pl.when(f < fines - 1)
+    def _():
+        signal(barrier, fine=f + 1)
+
+    inner = jnp.logical_and(f > 0, f < fines - 1).astype(jnp.int32)
+    pl.semaphore_wait(barrier, channels + inner)
+
+    @pl.when(f == 0)
+    def _():
+        signal(ready.at[0], fine=f + 1)
+
+    @pl.when(f == fines - 1)
+    def _():
+        signal(ready.at[2], fine=f - 1)
 
     started = []
 
@@ -61,14 +84,24 @@
     def piece_start(half, p):
         return pl.multiple_of((half * half_rows + p * piece_rows) * chunks, 8)
 
-    halos = [
-        send(edge.at[0], hraw.at[0], edge_send.at[0], edge_recv.at[0], after_id),
-        send(edge.at[1], hraw.at[1], edge_send.at[1], edge_recv.at[1], before_id),
-    ]
-    theirs = 1 - mine
+    fetch.wait()
+    edge[0] = x_ref[pl.ds(chunks - 1, rows, stride=chunks), :]
+    edge[1] = x_ref[pl.ds(0, rows, stride=chunks), :]
     a_copies = [
         send(x_ref.at[pl.ds(piece_start(theirs, p), size), :], part_a.at[p], a_send.at[p], a_recv.at[p], partner)
-        for p in range(PIECES)
+        for p in range(1)
+    ]
+    edge_copy = send(edge, edge_a, a_send.at[PIECES], a_recv.at[PIECES], partner)
+    a_copies += [
+        send(x_ref.at[pl.ds(piece_start(theirs, p), size), :], part_a.at[p], a_send.at[p], a_recv.at[p], partner)
+        for p in range(1, PIECES)
+    ]
+
+    edge_copy.wait_recv()
+    edge_1[...] = edge[...] + edge_a[...]
+    edge_b_copies = [
+        send(edge_1, edge_b.at[o], b_send.at[o, PIECES], b_recv.at[o, PIECES], peers[o])
+        for o in range(others)
     ]
     b_copies = []
     for p in range(PIECES):
@@ -78,18 +111,48 @@
             send(sum_1.at[p], part_b.at[o, p], b_send.at[o, p], b_recv.at[o, p], peers[o])
             for o in range(others)
         ])
-    for copy in halos:
-        copy.wait_recv()
-    halo_pair = [
-        send(hraw.at[side, theirs], halo_a.at[side], a_send.at[PIECES + side], a_recv.at[PIECES + side], partner)
+
+    @pl.when(f > 0)
+    def _():
+        pl.semaphore_wait(ready.at[0], 1)
+
+    @pl.when(jnp.logical_and(f > 0, f < fines - 1))
+    def _():
+        signal(ready.at[0], fine=f + 1)
+
+    @pl.when(f == fines - 1)
+    def _():
+        signal(ready.at[1], coarse=prev_c)
+
+    @pl.when(f < fines - 1)
+    def _():
+        pl.semaphore_wait(ready.at[2], 1)
+
+    @pl.when(jnp.logical_and(f > 0, f < fines - 1))
+    def _():
+        signal(ready.at[2], fine=f - 1)
+
+    @pl.when(f == 0)
+    def _():
+        signal(ready.at[3], coarse=next_c)
+
+    total = edge_1[...]
+    for o in range(others):
+        edge_b_copies[o].wait_recv()
+        total = total + edge_b[o]
+    edge_n[...] = edge[...] * (1.0 / (total / channels)) - 1.0
+
+    @pl.when(f == fines - 1)
+    def _():
+        pl.semaphore_wait(ready.at[1], 1)
+
+    @pl.when(f == 0)
+    def _():
+        pl.semaphore_wait(ready.at[3], 1)
+
+    halo_copies = [
+        send(edge_n.at[side], halo.at[side], h_send.at[side], h_recv.at[side], around[side])
         for side in range(2)
-    ]
-    for side in range(2):
-        halo_pair[side].wait_recv()
-        halo_1[side] = hraw[side, mine] + halo_a[side]
-    halo_b_copies = [
-        send(halo_1, halo_b.at[o], b_send.at[o, PIECES], b_recv.at[o, PIECES], peers[o])
-        for o in range(others)
     ]
 
     def put(half, p, inverse):
@@ -107,30 +170,17 @@
         inv_1[p] = 1.0 / (total / channels)
         c_copies.append(send(inv_1.at[p], part_c.at[p], c_send.at[p], c_recv.at[p], partner))
         put(mine, p, inv_1[p])
-    total = halo_1[...]
-    for o in range(others):
-        halo_b_copies[o].wait_recv()
-        total = total + halo_b[o]
-    halo_i[...] = 1.0 / (total / channels)
-    halo_c_copy = send(halo_i, halo_c, c_send.at[PIECES], c_recv.at[PIECES], partner)
-
-    at_edge = [place == 0, place == channels * fines - 1]
-    at_row = [HEAD - 1, HEAD + chunks]
-
-    def put_halo(half, inverse):
-        for side in range(2):
-            normed = hraw[side, half] * inverse[side] - 1.0
-            normed = jnp.where(at_edge[side], jnp.zeros_like(normed), normed)
-            for i in range(half_rows):
-                t = half * half_rows + i
-                e_ref[pl.ds(t * ROW + at_row[side], 1), :] = normed[i : i + 1]
-
-    put_halo(mine, halo_i)
     for p in range(PIECES):
         c_copies[p].wait_recv()
         put(theirs, p, part_c[p])
-    halo_c_copy.wait_recv()
-    put_halo(theirs, halo_c)
+
+    at_end = [place == 0, place == channels * fines - 1]
+    at_row = [HEAD - 1, HEAD + chunks]
+    for side in range(2):
+        halo_copies[side].wait_recv()
+        normed = jnp.where(at_end[side], jnp.zeros((rows, LANES), jnp.float32), halo[side])
+        for t in range(rows):
+            e_ref[pl.ds(t * ROW + at_row[side], 1), :] = normed[t : t + 1]
     for copy in started:
         copy.wait_send()
 
@@ -241,20 +291,21 @@
     size = half // PIECES * chunks
     vmem = functools.partial(pltpu.VMEM, dtype=jnp.float32)
     dma = pltpu.SemaphoreType.DMA
-    x = spectra.reshape(rows * chunks, LANES)
+    x = pltpu.with_memory_space_constraint(spectra.reshape(rows * chunks, LANES), pltpu.HBM)
     normed = pl.pallas_call(
         functools.partial(comm_kernel, channels, fines, rows, chunks),
         out_shape=jax.ShapeDtypeStruct((rows * ROW, LANES), jnp.float32),
-        in_specs=[pl.BlockSpec(memory_space=pltpu.VMEM)],
+        in_specs=[pl.BlockSpec(memory_space=pltpu.HBM)],
         out_specs=pl.BlockSpec(memory_space=pltpu.VMEM),
         scratch_shapes=[
-            vmem((2, 2, half, LANES)), vmem((2, 2, half, LANES)),
+            vmem((rows * chunks, LANES)),
+            vmem((2, rows, LANES)), vmem((2, rows, LANES)), vmem((2, rows, LANES)),
+            vmem((others, 2, rows, LANES)), vmem((2, rows, LANES)), vmem((2, rows, LANES)),
             vmem((PIECES, size, LANES)), vmem((PIECES, size, LANES)),
             vmem((others, PIECES, size, LANES)), vmem((PIECES, size, LANES)), vmem((PIECES, size, LANES)),
-            vmem((2, half, LANES)), vmem((2, half, LANES)), vmem((others, 2, half, LANES)),
-            vmem((2, half, LANES)), vmem((2, half, LANES)),
-            dma((2,)), dma((2,)), dma((PIECES + 2,)), dma((PIECES + 2,)),
-            dma((others, PIECES + 1)), dma((others, PIECES + 1)), dma((PIECES + 1,)), dma((PIECES + 1,)),
+            dma, dma((PIECES + 1,)), dma((PIECES + 1,)),
+            dma((others, PIECES + 1)), dma((others, PIECES + 1)), dma((PIECES,)), dma((PIECES,)),
+            dma((2,)), dma((2,)), pltpu.SemaphoreType.REGULAR((4,)),
         ],
         compiler_params=pltpu.CompilerParams(collective_id=0, has_side_effects=True, vmem_limit_bytes=8 << 20),
         name="normalize",

time: 17.8 us -> 16.4 us (0.921)
  local copies, waits for them, and re-layouts: 0.95 us -> 0 us
  Pallas kernels: 16.7 us -> 16.3 us
    unnamed x2 -> x0, local copies, waits for them, and re-layouts: 0.95 us -> none
    pallas_call x1, Pallas kernels: 12.5 us -> 12.1 us  [on_device(): pl.pallas_call(functools.partial(comm_kernel, channels, fines, rows, chun...]
where the time goes in v2:
time: 16.4 us; the launch traced here: 16.3 us
  Pallas kernels  16.3 us (99%)
    pallas_call x1, Pallas kernels, on_device(): pl.pallas_call(functools.partial(comm_kernel, channels, fines, rows, chun...  12.1 us
    pallas_call x1, Pallas kernels, on_device(): pl.pallas_call(functools.partial(tree_kernel, channels, fines, rows, chun...  4.18 us

profile of v2, /device:TPU:0, one launch (start us, length us, event | category | flops | bytes accessed | tf_op | source)
XLA Modules:
  0.0 16.3 jit_solution(18404097797054717988)
XLA Ops:
  0.0 12.1 %normalize.1.e_ref = f32[576,128]{1,0:T(8,128)S(1)} custom-call(f32[512,128]{1,0:T(8,128)} %bitcast.2), custom_call_target="tpu_custom_call" | custom-call | tf_op jit(solution)/shard_map/normalize/pallas_call | solution.py:295
  12.1 4.2 %tree.1 = f32[8,512,128]{2,1,0:T(8,128)} custom-call(f32[576,128]{1,0:T(8,128)S(1)} %normalize.1.e_ref), custom_call_target="tpu_custom_call" | custom-call | tf_op jit(solution)/shard_map/tree/pallas_call | solution.py:314

commit v3 on v2

--- a/solution.py
+++ b/solution.py
@@ -87,16 +87,11 @@
     fetch.wait()
     edge[0] = x_ref[pl.ds(chunks - 1, rows, stride=chunks), :]
     edge[1] = x_ref[pl.ds(0, rows, stride=chunks), :]
+    edge_copy = send(edge, edge_a, a_send.at[PIECES], a_recv.at[PIECES], partner)
     a_copies = [
         send(x_ref.at[pl.ds(piece_start(theirs, p), size), :], part_a.at[p], a_send.at[p], a_recv.at[p], partner)
-        for p in range(1)
+        for p in range(PIECES)
     ]
-    edge_copy = send(edge, edge_a, a_send.at[PIECES], a_recv.at[PIECES], partner)
-    a_copies += [
-        send(x_ref.at[pl.ds(piece_start(theirs, p), size), :], part_a.at[p], a_send.at[p], a_recv.at[p], partner)
-        for p in range(1, PIECES)
-    ]
-
     edge_copy.wait_recv()
     edge_1[...] = edge[...] + edge_a[...]
     edge_b_copies = [
@@ -169,11 +164,8 @@
             total = total + part_b[o, p]
         inv_1[p] = 1.0 / (total / channels)
         c_copies.append(send(inv_1.at[p], part_c.at[p], c_send.at[p], c_recv.at[p], partner))
+    for p in range(PIECES):
         put(mine, p, inv_1[p])
-    for p in range(PIECES):
-        c_copies[p].wait_recv()
-        put(theirs, p, part_c[p])
-
     at_end = [place == 0, place == channels * fines - 1]
     at_row = [HEAD - 1, HEAD + chunks]
     for side in range(2):
@@ -181,6 +173,10 @@
         normed = jnp.where(at_end[side], jnp.zeros((rows, LANES), jnp.float32), halo[side])
         for t in range(rows):
             e_ref[pl.ds(t * ROW + at_row[side], 1), :] = normed[t : t + 1]
+    for p in range(PIECES):
+        c_copies[p].wait_recv()
+        put(theirs, p, part_c[p])
+
     for copy in started:
         copy.wait_send()
 

time: 16.4 us -> 16.4 us (level)
  no operation moved by 1% of the time
where the time goes in v3:
time: 16.4 us; the launch traced here: 16.3 us
  Pallas kernels  16.3 us (99%)
    pallas_call x1, Pallas kernels, on_device(): pl.pallas_call(functools.partial(comm_kernel, channels, fines, rows, chun...  12.1 us
    pallas_call x1, Pallas kernels, on_device(): pl.pallas_call(functools.partial(tree_kernel, channels, fines, rows, chun...  4.18 us

profile of v3, /device:TPU:0, one launch (start us, length us, event | category | flops | bytes accessed | tf_op | source)
XLA Modules:
  0.0 16.3 jit_solution(10057589547064258885)
XLA Ops:
  0.0 12.1 %normalize.1.e_ref = f32[576,128]{1,0:T(8,128)S(1)} custom-call(f32[512,128]{1,0:T(8,128)} %bitcast.2), custom_call_target="tpu_custom_call" | custom-call | tf_op jit(solution)/shard_map/normalize/pallas_call | solution.py:291
  12.1 4.2 %tree.1 = f32[8,512,128]{2,1,0:T(8,128)} custom-call(f32[576,128]{1,0:T(8,128)S(1)} %normalize.1.e_ref), custom_call_target="tpu_custom_call" | custom-call | tf_op jit(solution)/shard_map/tree/pallas_call | solution.py:310
